TPU v7x, 256 devices: a whole 4x4x8 slice. The times are simulated.
256 devices in a mesh: pb: 16 (over x, z_hi), sa: 16 (over z_lo, y, core).
Axes of the slice: x: 4, y: 4, z: 8 (z_hi: 4, z_lo: 2; z = z_hi * 2 + z_lo), core: 2. Of those that a mesh axis runs over, the one named last changes fastest.
Arguments:
- question_states: bfloat16 [16, 16, 256, 768], P('pb', 'sa'), may hold values from -16 to 16
- question_ids: int32 [16, 16, 256], P('pb'), may hold values from 0 to 30521, as said below
- q_inner_weight: bfloat16 [768, 3072], P(None, 'sa'), may hold values from -0.21875 to 0.21875
- q_outer_weight: bfloat16 [3072, 768], P('sa'), may hold values from -0.109375 to 0.109375
- q_norm_gain: float32 [768], replicated, may hold values from 0.1 to 1.9
- sql_states: bfloat16 [16, 16, 256, 768], P('sa', 'pb'), may hold values from -16 to 16
- sql_ids: int32 [16, 16, 256], P('sa'), may hold values from 0 to 32099, as said below
- s_inner_weight: bfloat16 [768, 3072], P(None, 'pb'), may hold values from -0.21875 to 0.21875
- s_outer_weight: bfloat16 [3072, 768], P('pb'), may hold values from -0.109375 to 0.109375
- s_norm_gain: float32 [768], replicated, may hold values from 0.1 to 1.9
- positive_column: int32 [256], P('pb'), may hold values from 0 to 255, each once
Outputs:
- loss: float32 [], replicated
- q_inner_grad: float32 [768, 3072], P(None, 'sa')
- q_outer_grad: float32 [3072, 768], P('sa')
- q_gain_grad: float32 [768], replicated
- s_inner_grad: float32 [768, 3072], P(None, 'pb')
- s_outer_grad: float32 [3072, 768], P('pb')
- s_gain_grad: float32 [768], replicated
Inputs may be any that keep to these rules, and one draw needn't show every extreme that they name: `question_ids`: each sequence is a run of nonzero ids followed by padding zeros, the run 3 * 64 long or longer. `sql_ids`: each sequence is a run of nonzero ids followed by padding zeros, the run 3 * 64 long or longer.
All inputs are finite; a program needn't handle non-finite values.
Results may differ from a plain program's by a relative error of at most 0.0051.
Values may be sent and summed in bfloat16 or wider, within the bound.
A program may use at most 128 MiB of HBM per device.

v0:
```python
import math
import jax
import jax.numpy as jnp
from jax import lax
from jax.sharding import PartitionSpec as P

D = 768
HIGH = lax.Precision.HIGHEST


def apply_rms_norm(input_float, norm_gain_vector, root_mean_square):
    if root_mean_square:
        input_normalized = input_float * lax.rsqrt(
            jnp.mean(input_float * input_float, axis=-1, keepdims=True) + 1e-06
        )
    else:
        mean_removed = input_float - jnp.mean(input_float, axis=-1, keepdims=True)
        input_normalized = mean_removed * lax.rsqrt(
            jnp.mean(mean_removed * mean_removed, axis=-1, keepdims=True) + 1e-05
        )
    return (input_normalized, (input_normalized * norm_gain_vector).astype(jnp.bfloat16))


def gelu_value(v):
    return 0.5 * v * (1.0 + lax.erf(v / math.sqrt(2.0)))


def gelu_slope(v):
    return 0.5 * (1.0 + lax.erf(v / math.sqrt(2.0))) + v * jnp.exp(-0.5 * v * v) / math.sqrt(
        2.0 * math.pi
    )


def pool_weights(ids):
    mask = (ids > 0).astype(jnp.float32)
    return mask / jnp.sum(mask, axis=-1, keepdims=True)


def forward_block(states, ids, inner, norm_gain_vector, root_mean_square):
    count, length, width = states.shape
    input_float = states.astype(jnp.float32).reshape(count * length, width)
    input_normalized, normalized_rows = apply_rms_norm(
        input_float, norm_gain_vector, root_mean_square
    )
    pre = jnp.dot(normalized_rows, inner, preferred_element_type=jnp.float32)
    hidden = gelu_value(pre).reshape(count, length, -1)
    return jnp.einsum("nt,ntf->nf", pool_weights(ids), hidden, precision=HIGH)


def residual_pool(states, ids):
    return jnp.einsum("nt,ntd->nd", pool_weights(ids), states.astype(jnp.float32), precision=HIGH)


def backward_block(states, ids, inner, norm_gain_vector, root_mean_square, hidden_grad):
    count, length, width = states.shape
    input_float = states.astype(jnp.float32).reshape(count * length, width)
    input_normalized, normalized_rows = apply_rms_norm(
        input_float, norm_gain_vector, root_mean_square
    )
    pre = jnp.dot(normalized_rows, inner, preferred_element_type=jnp.float32)
    weights = pool_weights(ids)
    slope = gelu_slope(pre).reshape(count, length, -1)
    dpre = (
        (weights[:, :, None] * hidden_grad[:, None, :] * slope)
        .reshape(count * length, -1)
        .astype(jnp.bfloat16)
    )
    inner_layer_grad = lax.dot_general(
        normalized_rows, dpre, (((0,), (0,)), ((), ())), preferred_element_type=jnp.float32
    )
    normalized_grad = lax.dot_general(
        dpre, inner, (((1,), (1,)), ((), ())), preferred_element_type=jnp.float32
    )
    return (inner_layer_grad, jnp.sum(input_normalized * normalized_grad, axis=0))


def per_device(
    question_states,
    question_ids,
    q_inner_weight,
    q_outer_weight,
    q_norm_gain,
    sql_states,
    sql_ids,
    s_inner_weight,
    s_outer_weight,
    s_norm_gain,
    positive_column,
):
    scale = 1.0 / math.sqrt(D)
    q_table = question_ids[0]
    s_table = sql_ids[0]
    q_rows = q_table.shape[0]
    s_rows = s_table.shape[0]
    own_count = question_states.shape[1]
    q_place = lax.axis_index("sa")
    s_place = lax.axis_index("pb")

    def s_forward(piece):
        pooled = forward_block(piece[0], s_table, s_inner_weight, s_norm_gain, True)
        return pooled

    ids = q_table
    pooled = forward_block(
        lax.all_gather(question_states, "sa", axis=1, tiled=True)[0],
        ids,
        q_inner_weight,
        q_norm_gain,
        False,
    )
    s_pooled = s_forward(lax.all_gather(sql_states, "pb", axis=1, tiled=True))
    q_first = q_place * own_count
    s_first = s_place * own_count
    q_own = residual_pool(
        question_states[0], lax.dynamic_slice_in_dim(q_table, q_first, own_count, 0)
    )
    s_own = residual_pool(sql_states[0], lax.dynamic_slice_in_dim(s_table, s_first, own_count, 0))
    q_resid = lax.dynamic_update_slice_in_dim(
        jnp.zeros((q_rows, D), jnp.float32), q_own, q_first, 0
    )
    s_resid = lax.dynamic_update_slice_in_dim(
        jnp.zeros((s_rows, D), jnp.float32), s_own, s_first, 0
    )
    q_outer_f = q_outer_weight.astype(jnp.float32)
    s_outer_f = s_outer_weight.astype(jnp.float32)
    q_embed = lax.psum(jnp.dot(pooled, q_outer_f, precision=HIGH) + q_resid, "sa")
    s_embed = lax.psum(jnp.dot(s_pooled, s_outer_f, precision=HIGH) + s_resid, "pb")
    tile = scale * lax.dot_general(q_embed, s_embed, (((1,), (1,)), ((), ())), precision=HIGH)
    columns = q_place * s_rows + jnp.arange(s_rows, dtype=jnp.int32)
    match = (positive_column[:, None] == columns[None, :]).astype(jnp.float32)
    row_top = lax.pmax(jnp.max(tile, axis=1), "sa")
    row_total, row_pos = lax.psum(
        (jnp.sum(jnp.exp(tile - row_top[:, None]), axis=1), jnp.sum(match * tile, axis=1)), "sa"
    )
    col_top = lax.pmax(jnp.max(tile, axis=0), "pb")
    col_total, col_pos = lax.psum(
        (jnp.sum(jnp.exp(tile - col_top[None, :]), axis=0), jnp.sum(match * tile, axis=0)), "pb"
    )
    row_lse = row_top + jnp.log(row_total)
    col_lse = col_top + jnp.log(col_total)
    pairs = q_rows * lax.axis_size("pb")
    row_part = jnp.where(q_place == 0, jnp.sum(row_lse - row_pos), 0.0)
    col_part = jnp.where(s_place == 0, jnp.sum(col_lse - col_pos), 0.0)
    loss_part = (row_part + col_part) / (2.0 * pairs)
    dscore = 0.5 * (
        jnp.exp(tile - row_lse[:, None]) + jnp.exp(tile - col_lse[None, :]) - 2.0 * match
    )
    q_grad = lax.psum(scale * jnp.dot(dscore, s_embed, precision=HIGH), "sa")
    s_grad = lax.psum(
        scale * lax.dot_general(dscore, q_embed, (((0,), (0,)), ((), ())), precision=HIGH), "pb"
    )
    q_outer_part = lax.dot_general(pooled, q_grad, (((0,), (0,)), ((), ())), precision=HIGH)
    s_outer_part = lax.dot_general(s_pooled, s_grad, (((0,), (0,)), ((), ())), precision=HIGH)
    q_hidden_grad = lax.dot_general(q_grad, q_outer_f, (((1,), (1,)), ((), ())), precision=HIGH)
    s_hidden_grad = lax.dot_general(s_grad, s_outer_f, (((1,), (1,)), ((), ())), precision=HIGH)

    def s_backward(piece):
        inner_layer_grad, gain_grad = backward_block(
            piece[0], s_table, s_inner_weight, s_norm_gain, True, s_hidden_grad
        )
        return (inner_layer_grad, gain_grad)

    ids = q_table
    inner_layer_grad, gain_grad = backward_block(
        lax.all_gather(question_states, "sa", axis=1, tiled=True)[0],
        ids,
        q_inner_weight,
        q_norm_gain,
        False,
        q_hidden_grad,
    )
    s_inner_part, s_gain_part = s_backward(lax.all_gather(sql_states, "pb", axis=1, tiled=True))
    q_inner_grad, q_outer_grad = lax.psum((inner_layer_grad, q_outer_part), "pb")
    s_inner_grad, s_outer_grad = lax.psum((s_inner_part, s_outer_part), "sa")
    q_gain_grad, s_gain_grad, loss = lax.psum((gain_grad, s_gain_part, loss_part), ("pb", "sa"))
    return (loss, q_inner_grad, q_outer_grad, q_gain_grad, s_inner_grad, s_outer_grad, s_gain_grad)


def solution(mesh):
    placed = (
        P("pb", "sa", None, None),
        P("pb", None, None),
        P(None, "sa"),
        P("sa", None),
        P(),
        P("sa", "pb", None, None),
        P("sa", None, None),
        P(None, "pb"),
        P("pb", None),
        P(),
        P("pb"),
    )
    return jax.shard_map(
        per_device,
        mesh=mesh,
        in_specs=placed,
        out_specs=(P(), P(None, "sa"), P("sa", None), P(), P(None, "pb"), P("pb", None), P()),
        check_vma=False,
    )
```

profile of v0, /device:TPU:1, one launch (start us, length us, event | category | flops | bytes accessed | tf_op | source)
XLA Modules:
  0.0 849.9 jit_solution(1982385561405561287)
XLA Ops:
  15.7 43.4 %all-gather.3.cloned.1.call-done = bf16[1,16,256,768]{3,2,0,1:T(8,128)(2,1)} async-done(((bf16[1,1,256,768]{3,2,0,1:T(8,128)(2,1)}), bf16[1,16,256,768]{3,2,0,1:T(8,128)(2,1)}) %all-gather.3.cloned.1.call-update) | async-done | bytes 6291472 | tf_op jit(solution)/shard_map/all_gather | solution.py:105
  59.1 3.8 convert_reduce_fusion
  63.7 1.9 multiply_reduce_fusion.3
  65.7 2.2 multiply_convert_fusion.1
  67.9 2.5 multiply_multiply_fusion.3
  70.5 2.7 fusion.16
  74.9 56.9 %psum.105 = f32[16,768]{1,0:T(8,128)S(1)} all-reduce(f32[16,768]{1,0:T(8,128)S(1)} %add.105), channel_id=1, replica_groups=mesh['pb'=16,'sa'=16] {'sa'}, use_global_device_ids=true, to_apply=%region_4.0 | all-reduce | flops 12288 | bytes 98304 | tf_op jit(solution)/shard_map/psum | solution.py:126
  131.7 27.8 %all-gather.5.cloned.1.call-done = bf16[1,16,256,768]{3,2,0,1:T(8,128)(2,1)} async-done(((bf16[1,1,256,768]{3,2,0,1:T(8,128)(2,1)}), bf16[1,16,256,768]{3,2,0,1:T(8,128)(2,1)}) %all-gather.5.cloned.1.call-update) | async-done | bytes 6291472 | tf_op jit(solution)/shard_map/all_gather | solution.py:111
  159.5 4.2 multiply_reduce_fusion.2
  165.9 3.6 multiply_multiply_fusion.2
  169.6 2.7 fusion.13
  174.8 67.6 %psum.106 = f32[16,768]{1,0:T(8,128)} all-reduce(f32[16,768]{1,0:T(8,128)S(1)} %add.109), channel_id=1, replica_groups=mesh['pb'=16,'sa'=16] {'pb'}, use_global_device_ids=true, to_apply=%region_8.0 | all-reduce | flops 12288 | bytes 98304 | tf_op jit(solution)/shard_map/psum | solution.py:127
  243.6 41.3 %pmax.14 = f32[16]{0:T(128)S(1)} all-reduce(f32[16]{0:T(128)S(1)} %get-tuple-element.12), channel_id=1, replica_groups=mesh['pb'=16,'sa'=16] {'sa'}, use_global_device_ids=true, to_apply=%region_10.0 | all-reduce | flops 16 | bytes 128 | tf_op jit(solution)/shard_map/pmax | solution.py:131
  284.9 32.1 %pmax.15 = f32[16]{0:T(128)S(1)} all-reduce(f32[16]{0:T(128)S(1)} %get-tuple-element.11), channel_id=1, replica_groups=mesh['pb'=16,'sa'=16] {'pb'}, use_global_device_ids=true, to_apply=%region_17.0 | all-reduce | flops 16 | bytes 128 | tf_op jit(solution)/shard_map/pmax | solution.py:135
  318.3 34.1 %psum.107 = f32[16]{0:T(128)S(1)} all-reduce(f32[16]{0:T(128)S(1)} %get-tuple-element.10), channel_id=1, replica_groups=mesh['pb'=16,'sa'=16] {'sa'}, use_global_device_ids=true, to_apply=%region_12.0 | all-reduce | flops 16 | bytes 128 | tf_op jit(solution)/shard_map/psum | solution.py:132
  352.4 34.7 %psum.109 = f32[16]{0:T(128)S(1)} all-reduce(f32[16]{0:T(128)S(1)} %get-tuple-element.9), channel_id=1, replica_groups=mesh['pb'=16,'sa'=16] {'pb'}, use_global_device_ids=true, to_apply=%region_19.0 | all-reduce | flops 16 | bytes 128 | tf_op jit(solution)/shard_map/psum | solution.py:136
  390.5 56.9 %all-reduce.1 = (f32[16]{0:T(128)}, f32[16,768]{1,0:T(8,128)S(1)}) all-reduce(f32[16]{0:T(128)} %get-tuple-element.8, f32[16,768]{1,0:T(8,128)} %convolution_multiply_fusion.1), channel_id=1, replica_groups=mesh['pb'=16,'sa'=16] {'sa'}, use_global_device_ids=true, to_apply=%region_14.0 | all-reduce | flops 12304 | bytes 98432 | tf_op jit(solution)/shard_map/psum | solution.py:132
  448.7 2.2 fusion.29
  451.4 4.4 copy.39
  455.8 63.2 %all-reduce.3 = (f32[16]{0:T(128)}, f32[16,768]{1,0:T(8,128)S(1)}) all-reduce(f32[16]{0:T(128)} %get-tuple-element.7, f32[16,768]{1,0:T(8,128)S(1)} %copy-done.27), channel_id=1, replica_groups=mesh['pb'=16,'sa'=16] {'pb'}, use_global_device_ids=true, to_apply=%region_21.0 | all-reduce | flops 12304 | bytes 98432 | tf_op jit(solution)/shard_map/psum | solution.py:136
  520.8 4.5 copy.42
  527.9 2.2 fusion.65
  530.3 2.8 fusion.12
  534.6 5.0 fusion.66
  539.8 5.9 multiply_reduce_fusion
  548.2 4.8 multiply_reduce_fusion.1
  553.1 89.9 %all-reduce = (f32[]{:T(128)}, f32[768]{0:T(1024)}, f32[768]{0:T(1024)}) all-reduce(f32[]{:T(128)S(6)} %div.107, f32[768]{0:T(1024)S(1)} %multiply_reduce_fusion.1, f32[768]{0:T(1024)S(1)} %multiply_reduce_fusion), channel_id=1, replica_groups=mesh['pb'=16,'sa'=16] {'pb','sa'}, use_global_device_ids=true, to_apply=%region_23.24 | all-reduce | flops 1537 | bytes 12296 | tf_op jit(solution)/shard_map/psum | solution.py:175
  643.0 57.8 %all-reduce.10.cloned.1.call-done = (f32[768,192]{0,1:T(8,128)}, f32[192,768]{1,0:T(8,128)}) async-done(((f32[768,192]{0,1:T(8,128)}, f32[192,768]{1,0:T(8,128)}), (f32[768,192]{0,1:T(8,128)}, f32[192,768]{1,0:T(8,128)})) %all-reduce.10.cloned.1.call-update) | async-done | bytes 1179664 | tf_op jit(solution)/shard_map/psum | solution.py:173
  700.8 135.9 %all-reduce.8.cloned.1.call-done = (f32[768,192]{0,1:T(8,128)}, f32[192,768]{1,0:T(8,128)}) async-done(((f32[768,192]{0,1:T(8,128)}, f32[192,768]{1,0:T(8,128)}), (f32[768,192]{0,1:T(8,128)}, f32[192,768]{1,0:T(8,128)})) %all-reduce.8.cloned.1.call-update) | async-done | bytes 1179664 | tf_op jit(solution)/shard_map/psum | solution.py:174
  836.7 2.0 copy.77
  838.7 1.9 copy.78
  840.6 1.9 copy.79
  (127 shorter events, 30.0 us)
Async XLA Ops:
  7.2 158.7 %copy-start = (bf16[768,192]{0,1:T(8,128)(2,1)S(1)}, bf16[768,192]{0,1:T(8,128)(2,1)}, u32[]{:S(2)}) copy-start(bf16[768,192]{0,1:T(8,128)(2,1)} %param.18) | copy-start | bytes 884740
  7.2 51.9 %all-gather.3.cloned.1.call-start = ((), (), s32[]{:S(2)}) async-start(), calls=%async_computation | async-start | bytes 6684672 | tf_op jit(solution)/shard_map/all_gather | solution.py:105
  7.9 151.6 %all-gather.5.cloned.1.call-start = ((), (), s32[]{:S(2)}) async-start(), calls=%async_computation.1 | async-start | bytes 6684672 | tf_op jit(solution)/shard_map/all_gather | solution.py:111
  8.7 692.1 %all-reduce.10.cloned.1.call-start = ((), (), s32[]{:S(2)}) async-start(), calls=%async_computation.3 | async-start | bytes 2359296 | tf_op jit(solution)/shard_map/psum | solution.py:173
  59.1 4.6 copy-start.1
  67.9 2.6 copy-start.2
  70.5 2.7 copy-start.12
  70.5 3.3 copy-start.7
  131.7 32.7 %copy-start.29 = (f32[768]{0:T(1024)S(1)}, f32[768]{0:T(1024)}, u32[]{:S(2)}) copy-start(f32[768]{0:T(1024)} %param.20) | copy-start | bytes 9220
  159.5 4.9 copy-start.4
  165.9 3.7 copy-start.3
  165.9 3.7 copy-start.20
  169.6 2.7 copy-start.13
  169.6 2.9 copy-start.8
  352.4 38.1 %copy-start.34 = (f32[16]{0:T(128)}, f32[16]{0:T(128)S(1)}, u32[]{:S(2)}) copy-start(f32[16]{0:T(128)S(1)} %log_add_fusion.1) | copy-start | bytes 196
  387.1 3.3 copy-start.32
  451.4 4.4 copy-start.27
  520.7 4.6 copy-start.6
  520.7 4.6 copy-start.19
  520.8 7.1 slice-start
  525.3 2.6 slice-start.1
  530.2 306.5 %all-reduce.8.cloned.1.call-start = ((), (), s32[]{:S(2)}) async-start(), calls=%async_computation.2 | async-start | bytes 2359296 | tf_op jit(solution)/shard_map/psum | solution.py:174
  534.6 5.1 copy-start.26
  539.7 6.0 copy-start.30
  539.7 6.0 copy-start.35
  539.7 7.2 copy-start.31
  539.7 7.2 copy-start.33
  539.7 8.5 copy-start.10
  539.7 8.5 copy-start.16
  539.7 8.5 copy-start.22
  539.7 8.5 copy-start.24
  836.7 5.8 copy-start.14
  (10 other events, 17.2 us)
Sparse Core Ops, SparseCore 0:
  9.9 49.1 all-gather.2
  61.5 97.9 all-gather.4
  530.3 170.4 all-reduce.9
  703.9 132.7 all-reduce.7
where the time goes:
time: 851 us; the launch traced here: 850 us
  blocking collectives  477 us (56%)
  waiting for transfers between devices  266 us (31%)
  matrix products  43.3 us (5%)
  other arithmetic  26 us (3%)
  local copies, waits for them, and re-layouts  20.5 us (2%)
  between operations  17 us (2%)
    psum x1, waiting for transfers between devices, per_device(): s_inner_grad, s_outer_grad = lax.psum((s_inner_part, s_outer_part), 'sa')  136 us
    psum x2, blocking collectives, per_device(): lax.psum((jnp.sum(jnp.exp(tile - col_top[None, :]), axis=0), jnp.sum(matc...  97.9 us
    psum x2, blocking collectives, per_device(): lax.psum((jnp.sum(jnp.exp(tile - row_top[:, None]), axis=1), jnp.sum(matc...  91 us
    psum x1, blocking collectives, per_device(): lax.psum((gain_grad, s_gain_part, loss_part), ('pb', 'sa'))  89.9 us
    psum x1, blocking collectives, per_device(): lax.psum(jnp.dot(s_pooled, s_outer_f, precision=HIGH) + s_resid, 'pb')  67.6 us
    psum x1, waiting for transfers between devices, per_device(): lax.psum((inner_layer_grad, q_outer_part), 'pb')  57.8 us
    psum x1, blocking collectives, per_device(): lax.psum(jnp.dot(pooled, q_outer_f, precision=HIGH) + q_resid, 'sa')  56.9 us
    all_gather x1, waiting for transfers between devices, per_device(): lax.all_gather(question_states, 'sa', axis=1, tiled=True)[0]  43.4 us
  transfers between devices with their start and end apart: 4, of which 4 were waited for; matrix products, arithmetic and copies ran while one was open for 5% of the time, Pallas kernels for 0%

commit v1 on v0

--- a/solution.py
+++ b/solution.py
@@ -3,9 +3,15 @@
 import jax.numpy as jnp
 from jax import lax
 from jax.sharding import PartitionSpec as P
+from jax.lax import psum
 
 D = 768
 HIGH = lax.Precision.HIGHEST
+
+
+def outputs_serve(vector):
+    next_value = psum(vector, axis_name="pb")
+    return psum(next_value, axis_name="sa")
 
 
 def apply_rms_norm(input_float, norm_gain_vector, root_mean_square):
@@ -172,7 +178,7 @@
     s_inner_part, s_gain_part = s_backward(lax.all_gather(sql_states, "pb", axis=1, tiled=True))
     q_inner_grad, q_outer_grad = lax.psum((inner_layer_grad, q_outer_part), "pb")
     s_inner_grad, s_outer_grad = lax.psum((s_inner_part, s_outer_part), "sa")
-    q_gain_grad, s_gain_grad, loss = lax.psum((gain_grad, s_gain_part, loss_part), ("pb", "sa"))
+    q_gain_grad, s_gain_grad, loss = outputs_serve((gain_grad, s_gain_part, loss_part))
     return (loss, q_inner_grad, q_outer_grad, q_gain_grad, s_inner_grad, s_outer_grad, s_gain_grad)
 
 

time: 851 us -> 851 us (level)
    psum x1 -> x2, blocking collectives: 89.9 us -> 88.8 us  [the longest x1 53 us: outputs_serve(): return psum(next_value, axis_name='sa')]
where the time goes in v1:
time: 851 us; the launch traced here: 850 us
  blocking collectives  476 us (56%)
  waiting for transfers between devices  268 us (31%)
  matrix products  43.3 us (5%)
  other arithmetic  26 us (3%)
  local copies, waits for them, and re-layouts  20.5 us (2%)
  between operations  17 us (2%)
    psum x1, waiting for transfers between devices, per_device(): s_inner_grad, s_outer_grad = lax.psum((s_inner_part, s_outer_part), 'sa')  136 us
    psum x2, blocking collectives, per_device(): lax.psum((jnp.sum(jnp.exp(tile - col_top[None, :]), axis=0), jnp.sum(matc...  97.9 us
    psum x2, blocking collectives, per_device(): lax.psum((jnp.sum(jnp.exp(tile - row_top[:, None]), axis=1), jnp.sum(matc...  91 us
    psum x1, blocking collectives, per_device(): lax.psum(jnp.dot(s_pooled, s_outer_f, precision=HIGH) + s_resid, 'pb')  67.6 us
    psum x1, waiting for transfers between devices, per_device(): lax.psum((inner_layer_grad, q_outer_part), 'pb')  59.8 us
    psum x1, blocking collectives, per_device(): lax.psum(jnp.dot(pooled, q_outer_f, precision=HIGH) + q_resid, 'sa')  56.9 us
    psum x1, blocking collectives, outputs_serve(): return psum(next_value, axis_name='sa')  53 us
    all_gather x1, waiting for transfers between devices, per_device(): lax.all_gather(question_states, 'sa', axis=1, tiled=True)[0]  43.4 us
  transfers between devices with their start and end apart: 4, of which 4 were waited for; matrix products, arithmetic and copies ran while one was open for 5% of the time, Pallas kernels for 0%

profile of v1, /device:TPU:1, one launch (start us, length us, event | category | flops | bytes accessed | tf_op | source)
XLA Modules:
  0.0 850.4 jit_solution(10881665910788480222)
XLA Ops:
  15.7 43.4 %all-gather.3.cloned.1.call-done = bf16[1,16,256,768]{3,2,0,1:T(8,128)(2,1)} async-done(((bf16[1,1,256,768]{3,2,0,1:T(8,128)(2,1)}), bf16[1,16,256,768]{3,2,0,1:T(8,128)(2,1)}) %all-gather.3.cloned.1.call-update) | async-done | bytes 6291472 | tf_op jit(solution)/shard_map/all_gather | solution.py:111
  59.1 3.8 convert_reduce_fusion
  63.7 1.9 multiply_reduce_fusion.3
  65.7 2.2 multiply_convert_fusion.1
  67.9 2.5 multiply_multiply_fusion.3
  70.5 2.7 fusion.16
  74.9 56.9 %psum.126 = f32[16,768]{1,0:T(8,128)S(1)} all-reduce(f32[16,768]{1,0:T(8,128)S(1)} %add.111), channel_id=1, replica_groups=mesh['pb'=16,'sa'=16] {'sa'}, use_global_device_ids=true, to_apply=%region_4.0 | all-reduce | flops 12288 | bytes 98304 | tf_op jit(solution)/shard_map/psum | solution.py:132
  131.7 27.8 %all-gather.5.cloned.1.call-done = bf16[1,16,256,768]{3,2,0,1:T(8,128)(2,1)} async-done(((bf16[1,1,256,768]{3,2,0,1:T(8,128)(2,1)}), bf16[1,16,256,768]{3,2,0,1:T(8,128)(2,1)}) %all-gather.5.cloned.1.call-update) | async-done | bytes 6291472 | tf_op jit(solution)/shard_map/all_gather | solution.py:117
  159.5 4.2 multiply_reduce_fusion.2
  165.9 3.6 multiply_multiply_fusion.2
  169.6 2.7 fusion.13
  174.8 67.6 %psum.127 = f32[16,768]{1,0:T(8,128)} all-reduce(f32[16,768]{1,0:T(8,128)S(1)} %add.115), channel_id=1, replica_groups=mesh['pb'=16,'sa'=16] {'pb'}, use_global_device_ids=true, to_apply=%region_8.0 | all-reduce | flops 12288 | bytes 98304 | tf_op jit(solution)/shard_map/psum | solution.py:133
  243.6 41.3 %pmax.14 = f32[16]{0:T(128)S(1)} all-reduce(f32[16]{0:T(128)S(1)} %get-tuple-element.12), channel_id=1, replica_groups=mesh['pb'=16,'sa'=16] {'sa'}, use_global_device_ids=true, to_apply=%region_10.0 | all-reduce | flops 16 | bytes 128 | tf_op jit(solution)/shard_map/pmax | solution.py:137
  284.9 32.1 %pmax.15 = f32[16]{0:T(128)S(1)} all-reduce(f32[16]{0:T(128)S(1)} %get-tuple-element.11), channel_id=1, replica_groups=mesh['pb'=16,'sa'=16] {'pb'}, use_global_device_ids=true, to_apply=%region_17.0 | all-reduce | flops 16 | bytes 128 | tf_op jit(solution)/shard_map/pmax | solution.py:141
  318.3 34.1 %psum.128 = f32[16]{0:T(128)S(1)} all-reduce(f32[16]{0:T(128)S(1)} %get-tuple-element.10), channel_id=1, replica_groups=mesh['pb'=16,'sa'=16] {'sa'}, use_global_device_ids=true, to_apply=%region_12.0 | all-reduce | flops 16 | bytes 128 | tf_op jit(solution)/shard_map/psum | solution.py:138
  352.4 34.7 %psum.130 = f32[16]{0:T(128)S(1)} all-reduce(f32[16]{0:T(128)S(1)} %get-tuple-element.9), channel_id=1, replica_groups=mesh['pb'=16,'sa'=16] {'pb'}, use_global_device_ids=true, to_apply=%region_19.0 | all-reduce | flops 16 | bytes 128 | tf_op jit(solution)/shard_map/psum | solution.py:142
  390.5 56.9 %all-reduce.1 = (f32[16]{0:T(128)}, f32[16,768]{1,0:T(8,128)S(1)}) all-reduce(f32[16]{0:T(128)} %get-tuple-element.8, f32[16,768]{1,0:T(8,128)} %convolution_multiply_fusion.1), channel_id=1, replica_groups=mesh['pb'=16,'sa'=16] {'sa'}, use_global_device_ids=true, to_apply=%region_14.0 | all-reduce | flops 12304 | bytes 98432 | tf_op jit(solution)/shard_map/psum | solution.py:138
  448.7 2.2 fusion.29
  451.4 4.4 copy.39
  455.8 63.2 %all-reduce.4 = (f32[16]{0:T(128)}, f32[16,768]{1,0:T(8,128)S(1)}) all-reduce(f32[16]{0:T(128)} %get-tuple-element.7, f32[16,768]{1,0:T(8,128)S(1)} %copy-done.27), channel_id=1, replica_groups=mesh['pb'=16,'sa'=16] {'pb'}, use_global_device_ids=true, to_apply=%region_21.0 | all-reduce | flops 12304 | bytes 98432 | tf_op jit(solution)/shard_map/psum | solution.py:142
  520.8 4.5 copy.42
  527.9 2.2 fusion.65
  530.3 2.8 fusion.12
  534.6 5.0 fusion.66
  539.8 5.9 multiply_reduce_fusion
  548.2 4.8 multiply_reduce_fusion.1
  553.1 35.8 %all-reduce.3 = (f32[]{:T(128)}, f32[768]{0:T(1024)S(1)}, f32[768]{0:T(1024)S(1)}) all-reduce(f32[]{:T(128)S(6)} %div.107, f32[768]{0:T(1024)S(1)} %multiply_reduce_fusion.1, f32[768]{0:T(1024)S(1)} %multiply_reduce_fusion), channel_id=1, replica_groups=mesh['pb'=16,'sa'=16] {'pb'}, use_global_device_ids=true, to_apply=%region_23.24 | all-reduce | flops 1537 | bytes 12296 | tf_op jit(solution)/shard_map/psum | solution.py:13
  588.8 53.0 %all-reduce = (f32[]{:T(128)}, f32[768]{0:T(1024)}, f32[768]{0:T(1024)}) all-reduce(f32[]{:T(128)} %get-tuple-element.20, f32[768]{0:T(1024)S(1)} %get-tuple-element.21, f32[768]{0:T(1024)S(1)} %get-tuple-element.22), channel_id=1, replica_groups=mesh['pb'=16,'sa'=16] {'sa'}, use_global_device_ids=true, to_apply=%region_24.25 | all-reduce | flops 1537 | bytes 12296 | tf_op jit(solution)/shard_map/psum | solution.py:14
  641.9 59.8 %all-reduce.11.cloned.1.call-done = (f32[768,192]{0,1:T(8,128)}, f32[192,768]{1,0:T(8,128)}) async-done(((f32[768,192]{0,1:T(8,128)}, f32[192,768]{1,0:T(8,128)}), (f32[768,192]{0,1:T(8,128)}, f32[192,768]{1,0:T(8,128)})) %all-reduce.11.cloned.1.call-update) | async-done | bytes 1179664 | tf_op jit(solution)/shard_map/psum | solution.py:179
  701.7 135.5 %all-reduce.9.cloned.1.call-done = (f32[768,192]{0,1:T(8,128)}, f32[192,768]{1,0:T(8,128)}) async-done(((f32[768,192]{0,1:T(8,128)}, f32[192,768]{1,0:T(8,128)}), (f32[768,192]{0,1:T(8,128)}, f32[192,768]{1,0:T(8,128)})) %all-reduce.9.cloned.1.call-update) | async-done | bytes 1179664 | tf_op jit(solution)/shard_map/psum | solution.py:180
  837.2 2.0 copy.77
  839.2 1.9 copy.78
  (128 shorter events, 31.9 us)
Async XLA Ops:
  7.2 158.7 %copy-start = (bf16[768,192]{0,1:T(8,128)(2,1)S(1)}, bf16[768,192]{0,1:T(8,128)(2,1)}, u32[]{:S(2)}) copy-start(bf16[768,192]{0,1:T(8,128)(2,1)} %param.18) | copy-start | bytes 884740
  7.2 51.9 %all-gather.3.cloned.1.call-start = ((), (), s32[]{:S(2)}) async-start(), calls=%async_computation | async-start | bytes 6684672 | tf_op jit(solution)/shard_map/all_gather | solution.py:111
  7.9 151.6 %all-gather.5.cloned.1.call-start = ((), (), s32[]{:S(2)}) async-start(), calls=%async_computation.1 | async-start | bytes 6684672 | tf_op jit(solution)/shard_map/all_gather | solution.py:117
  8.7 693.0 %all-reduce.11.cloned.1.call-start = ((), (), s32[]{:S(2)}) async-start(), calls=%async_computation.3 | async-start | bytes 2359296 | tf_op jit(solution)/shard_map/psum | solution.py:179
  59.1 4.6 copy-start.1
  67.9 2.6 copy-start.2
  70.5 2.7 copy-start.12
  70.5 3.3 copy-start.7
  131.7 32.7 %copy-start.29 = (f32[768]{0:T(1024)S(1)}, f32[768]{0:T(1024)}, u32[]{:S(2)}) copy-start(f32[768]{0:T(1024)} %param.20) | copy-start | bytes 9220
  159.5 4.9 copy-start.4
  165.9 3.7 copy-start.3
  165.9 3.7 copy-start.20
  169.6 2.7 copy-start.13
  169.6 2.9 copy-start.8
  352.4 38.1 %copy-start.34 = (f32[16]{0:T(128)}, f32[16]{0:T(128)S(1)}, u32[]{:S(2)}) copy-start(f32[16]{0:T(128)S(1)} %log_add_fusion.1) | copy-start | bytes 196
  387.1 3.3 copy-start.32
  451.4 4.4 copy-start.27
  520.7 4.6 copy-start.6
  520.7 4.6 copy-start.19
  520.8 7.1 slice-start
  525.3 2.6 slice-start.1
  530.2 307.0 %all-reduce.9.cloned.1.call-start = ((), (), s32[]{:S(2)}) async-start(), calls=%async_computation.2 | async-start | bytes 2359296 | tf_op jit(solution)/shard_map/psum | solution.py:180
  534.6 5.1 copy-start.26
  539.7 6.0 copy-start.30
  539.7 6.0 copy-start.35
  539.7 7.2 copy-start.31
  539.7 7.2 copy-start.33
  539.7 8.5 copy-start.10
  539.7 8.5 copy-start.16
  539.7 8.5 copy-start.22
  539.7 8.5 copy-start.24
  837.2 5.8 copy-start.14
  (10 other events, 17.2 us)
Sparse Core Ops, SparseCore 0:
  9.9 49.1 all-gather.2
  61.5 97.9 all-gather.4
  530.3 171.2 all-reduce.10
  704.8 132.3 all-reduce.8
